TPU v7x, 256 devices: a whole 4x4x8 slice. The times are simulated.
256 devices in a mesh: ep: 32 (over x, z), tp: 8 (over y, core).
Axes of the slice: x: 4, y: 4, z: 8, core: 2. Of those that a mesh axis runs over, the one named last changes fastest.
Arguments:
- attn_out: bfloat16 [8192, 2048], P('ep', 'tp'), may hold values from -6 to 6
- out_proj: bfloat16 [2048, 2048], P('tp'), may hold values from -0.125 to 0.125
- residual: bfloat16 [8192, 2048], P('ep'), may hold values from -40 to 40
- norm_gain: float32 [2048], replicated, may hold values from 0.25 to 1.75
- router: bfloat16 [2048, 64], replicated, may hold values from -0.125 to 0.125
- expert_gate_up: bfloat16 [256, 2, 352, 2048], P(('ep', 'tp')), may hold values from -0.125 to 0.125
- expert_down: bfloat16 [256, 352, 2048], P(('ep', 'tp')), may hold values from -0.15625 to 0.15625
- shared_gate_up: bfloat16 [2, 2816, 2048], P(None, 'tp'), may hold values from -0.125 to 0.125
- shared_down: bfloat16 [2816, 2048], P('tp'), may hold values from -0.109375 to 0.109375
- routes: int32 [8192, 6], P('ep'), may hold values from 0 to 63, all different within a row; in each aligned block of 256 rows (0 to 255, 256 to 511, ...) at most 40 rows name the same one
- live_rows: int32 [32], P('ep'), may hold values from 128 to 256, as said below
- next_gain: float32 [2048], replicated, may hold values from 0.25 to 1.75
Outputs:
- next_stream: bfloat16 [8192, 2048], P('ep', 'tp')
- next_normed: bfloat16 [8192, 2048], P('ep', 'tp')
Inputs may be any that keep to these rules, and one draw needn't show every extreme that they name: `routes`: each row names 6 different experts. Among the 256 rows of one block no expert is named by more than 40 rows, a bound that some block reaches. The live rows of block b are its first live_rows[b] rows; in every draw some block is entirely live.
All inputs are finite; a program needn't handle non-finite values.
Results may differ from a plain program's by a relative error of at most 0.012.
Values may be sent and summed in bfloat16 or wider, within the bound.
A program may use at most 128 MiB of HBM per device.

v0:
```python
import jax
import jax.numpy as jnp
from jax import lax
from jax.sharding import PartitionSpec as P

EXP_DEV = 2
norm_epsilon = 1e-06
routed_scale = 2.446


def slot_table(route_block, live_count, experts, capacity):
    fanout = route_block.shape[1]
    flat_ids = route_block.reshape(-1)
    entry_index = jnp.arange(flat_ids.shape[0], dtype=jnp.int32)
    living = entry_index // fanout < live_count
    one_hot = (
        (flat_ids[:, None] == jnp.arange(experts, dtype=jnp.int32)[None, :]) & living[:, None]
    ).astype(jnp.int32)
    earlier = jnp.cumsum(one_hot, axis=0, dtype=jnp.int32) - one_hot
    position = jnp.sum(earlier * one_hot, axis=1, dtype=jnp.int32)
    slot_index = jnp.where(living, flat_ids * capacity + position, experts * capacity)
    slot_owner = (
        jnp.full((experts * capacity,), -1, jnp.int32).at[slot_index].set(entry_index, mode="drop")
    )
    return (slot_index, living, slot_owner)


def gate_weights(normed, router, route_block):
    logits = jnp.dot(normed, router, preferred_element_type=jnp.float32)
    chosen = jnp.take_along_axis(logits, route_block, axis=1)
    scores = jax.nn.sigmoid(chosen)
    return scores / jnp.sum(scores, axis=1, keepdims=True) * routed_scale


def on_device(
    attn_out,
    out_proj,
    residual,
    norm_gain,
    router,
    expert_gate_up,
    expert_down,
    shared_gate_up,
    shared_down,
    routes,
    live_rows,
    next_gain,
):
    partial_out = jnp.dot(attn_out, out_proj, preferred_element_type=jnp.float32)
    summed = lax.psum(partial_out, "tp")
    stream = (summed + residual.astype(jnp.float32)).astype(jnp.bfloat16)
    stream_wide = stream.astype(jnp.float32)
    normed = (
        stream_wide
        * lax.rsqrt(jnp.mean(stream_wide * stream_wide, axis=1, keepdims=True) + norm_epsilon)
        * norm_gain
    ).astype(jnp.bfloat16)
    width = normed.shape[1]
    tp_count = lax.axis_size("tp")
    ep_count = lax.axis_size("ep")
    width_slice = width // tp_count
    column_start = lax.axis_index("tp") * width_slice
    unit_blocks = tp_count // EXP_DEV
    group = lax.axis_index("tp") // unit_blocks
    experts = router.shape[1]
    fanout = routes.shape[1]
    token_rows = routes.shape[0]
    capacity = token_rows * fanout * 5 // (3 * experts)
    slot_index, living, slot_owner = slot_table(routes, live_rows[0], experts, capacity)
    owners = slot_owner.reshape(ep_count, EXP_DEV, capacity)
    filled = owners >= 0
    source_row = jnp.where(filled, owners // fanout, 0)
    dispatched = jnp.where(filled[:, :, :, None], normed[source_row], jnp.zeros((), jnp.bfloat16))
    rows = lax.dynamic_index_in_dim(
        lax.all_to_all(dispatched, "ep", split_axis=0, concat_axis=0, tiled=True),
        group,
        1,
        keepdims=False,
    )
    gate_proj = jnp.einsum(
        "scd,fd->scf", rows, expert_gate_up[0, 0], preferred_element_type=jnp.float32
    )
    up_proj = jnp.einsum(
        "scd,fd->scf", rows, expert_gate_up[0, 1], preferred_element_type=jnp.float32
    )
    hidden = (jax.nn.silu(gate_proj) * up_proj).astype(jnp.bfloat16)
    produced = jnp.einsum(
        "scf,fd->scd", hidden, expert_down[0], preferred_element_type=jnp.float32
    ).astype(jnp.bfloat16)
    returned = lax.all_to_all(produced, "ep", split_axis=0, concat_axis=0, tiled=True)
    flat_terms = returned.reshape(ep_count * capacity, width)
    living_pairs = living.reshape(token_rows, fanout)
    mine = living_pairs & (routes % EXP_DEV == group)
    position = slot_index.reshape(token_rows, fanout) - routes * capacity
    term_row = jnp.where(mine, routes // EXP_DEV * capacity + position, 0)
    weights = gate_weights(normed, router, routes) * mine.astype(jnp.float32)
    picked = flat_terms[term_row]
    routed_part = jnp.einsum("tkd,tk->td", picked.astype(jnp.float32), weights)
    shared_gate = jnp.einsum(
        "td,fd->tf", normed, shared_gate_up[0], preferred_element_type=jnp.float32
    )
    shared_up = jnp.einsum(
        "td,fd->tf", normed, shared_gate_up[1], preferred_element_type=jnp.float32
    )
    shared_hidden = (jax.nn.silu(shared_gate) * shared_up).astype(jnp.bfloat16)
    shared_part = jnp.dot(shared_hidden, shared_down, preferred_element_type=jnp.float32)
    combined = lax.psum_scatter(
        (routed_part + shared_part).astype(jnp.bfloat16), "tp", scatter_dimension=1, tiled=True
    ).astype(jnp.float32)
    stream_slice = lax.dynamic_slice_in_dim(stream, column_start, width_slice, 1)
    next_stream = (stream_slice.astype(jnp.float32) + combined).astype(jnp.bfloat16)
    next_wide = next_stream.astype(jnp.float32)
    squares = lax.psum(jnp.sum(next_wide * next_wide, axis=1), "tp")
    gain_slice = lax.dynamic_slice_in_dim(next_gain, column_start, width_slice, 0)
    next_normed = (
        next_wide * lax.rsqrt(squares[:, None] / width + norm_epsilon) * gain_slice
    ).astype(jnp.bfloat16)
    return (next_stream, next_normed)


def solution(mesh):
    in_specs = (
        P("ep", "tp"),
        P("tp", None),
        P("ep", None),
        P(),
        P(),
        P(("ep", "tp"), None, None, None),
        P(("ep", "tp"), None, None),
        P(None, "tp", None),
        P("tp", None),
        P("ep", None),
        P("ep"),
        P(),
    )
    out_specs = (P("ep", "tp"), P("ep", "tp"))
    return jax.shard_map(
        on_device, mesh=mesh, in_specs=in_specs, out_specs=out_specs, check_vma=False
    )
```

profile of v0, /device:TPU:1, one launch (start us, length us, event | category | flops | bytes accessed | tf_op | source)
XLA Modules:
  0.0 608.2 jit_solution(8504731297024068242)
XLA Ops:
  7.2 3.1 fusion.76
  11.6 18.1 %reduce-window.6 = s32[64,12,128]{2,1,0:T(8,128)S(1)} reduce-window(s32[64,12,128]{2,1,0:T(8,128)S(1)} %fusion.37, s32[]{:T(128)} %constant.103.clone.1), window={size=1x1x128 pad=0_0x0_0x127_0}, to_apply=%region_1.0 | reduce-window | flops 12484608 | bytes 786436 | tf_op jit(solution)/shard_map/reduce-window
  29.7 0.2 slice.30
  29.9 0.3 copy.44
  30.3 0.2 broadcast_add_fusion
  31.3 6.2 %scatter_custom_fusion = s32[2560]{0:T(1024)S(1)} fusion(s32[1536]{0:T(1024)S(1)} %fusion.67, s32[1536]{0:T(1024)S(1)} %iota.72, s32[]{:T(128)} %constant.107.clone.1), kind=kCustom, calls=%fused_computation.112 | custom fusion | bytes 10244 | tf_op jit(solution)/shard_map/scatter | solution.py:23
  37.7 0.7 ge.27
  38.8 0.6 pad_clamp_fusion
  39.4 44.1 %all-reduce.2.cloned.1.call-done = f32[256,2048]{1,0:T(8,128)} async-done(((f32[256,2048]{1,0:T(8,128)}), f32[256,2048]{1,0:T(8,128)}) %all-reduce.2.cloned.1.call-update) | async-done | bytes 2097168 | tf_op jit(solution)/shard_map/psum | solution.py:50
  83.4 2.3 fusion.7
  85.7 0.3 fusion.9
  86.0 10.9 %gather_fusion = bf16[2560,2048]{1,0:T(8,128)(2,1)} fusion(bf16[256,2048]{1,0:T(8,128)(2,1)S(1)} %fusion.9, s32[3072]{0:T(1024)} %pad_clamp_fusion), kind=kCustom, calls=%fused_computation | custom fusion | bytes 20981760 | tf_op jit(solution)/shard_map/gather | solution.py:73
  97.0 10.0 %broadcast_select_fusion = bf16[32,2,40,2048]{3,2,1,0:T(8,128)(2,1)} fusion(bf16[32,2,40,2048]{3,2,1,0:T(8,128)(2,1)} %bitcast.83, pred[32,2,40]{2,1,0:T(4,128)(4,1)} %ge.27), kind=kLoop, calls=%fused_computation.4 | loop fusion | flops 5242880 | bytes 20974080 | tf_op jit(solution)/shard_map/jit(_where)/select_n | solution.py:73
  106.9 9.7 %all-to-all-start = ((bf16[32,2,40,2048]{3,2,1,0:T(8,128)(2,1)}), bf16[32,2,40,2048]{3,2,1,0:T(8,128)(2,1)}, u32[]{:S(2)}, u32[]{:S(2)}) async-start(bf16[32,2,40,2048]{3,2,1,0:T(8,128)(2,1)} %broadcast_select_fusion), calls=%async_computation | async-start | bytes 20971520 | tf_op jit(solution)/shard_map/all_to_all | solution.py:75
  116.6 232.0 %all-to-all-done = bf16[32,2,40,2048]{3,2,1,0:T(8,128)(2,1)} async-done(((bf16[32,2,40,2048]{3,2,1,0:T(8,128)(2,1)}), bf16[32,2,40,2048]{3,2,1,0:T(8,128)(2,1)}, u32[]{:S(2)}, u32[]{:S(2)}) %all-to-all-start) | async-done | bytes 10485792 | tf_op jit(solution)/shard_map/all_to_all | solution.py:75
  348.6 7.1 %fusion.2 = f32[32,40,352]{2,1,0:T(8,128)} fusion(bf16[32,2,40,2048]{3,2,1,0:T(8,128)(2,1)} %all-to-all-done, s32[]{:T(128)S(6)} %select_n.135, bf16[1,2,352,2048]{3,2,1,0:T(8,128)(2,1)} %param.17), kind=kOutput, calls=%fused_computation.7 | convolution fusion | flops 1845493760 | bytes 8486916 | tf_op jit(solution)/shard_map/scd,fd->scf/dot_general | solution.py:80
  355.7 9.8 %convolution_convert_fusion = bf16[32,40,2048]{2,1,0:T(8,128)(2,1)} fusion(bf16[1,352,2048]{2,1,0:T(8,128)(2,1)S(1)} %copy-done, f32[32,40,352]{2,1,0:T(8,128)} %fusion.2, bf16[32,2,40,2048]{3,2,1,0:T(8,128)(2,1)} %all-to-all-done, s32[]{:T(128)S(6)} %select_n.135, bf16[1,2,352,2048]{3,2,1,0:T(8,128)(2,1)} %param.17), kind=kOutput, calls=%fused_computation.11 | convolution fusion | flops 3696312320 | bytes 15335428 | tf_op jit(solution)/shard_map/scf,fd->scd/dot_general | solution.py:87
  365.5 10.2 %all-to-all-start.1 = ((bf16[32,40,2048]{2,1,0:T(8,128)(2,1)}), bf16[32,40,2048]{2,1,0:T(8,128)(2,1)}, u32[]{:S(2)}, u32[]{:S(2)}) async-start(bf16[32,40,2048]{2,1,0:T(8,128)(2,1)} %convolution_convert_fusion), calls=%async_computation.1 | async-start | bytes 10485760 | tf_op jit(solution)/shard_map/all_to_all | solution.py:90
  375.7 0.2 reduce-scatter.2.cloned.1.call-start
  376.6 0.4 fusion.77
  377.0 12.7 %gather_fusion.2 = f32[1536]{0:T(1024)S(1)} fusion(f32[256,64]{0,1:T(8,128)S(1)} %fusion.77, s32[1536]{0:T(1024)S(1)} %reshape.237), kind=kCustom, calls=%fused_computation.2 | custom fusion | bytes 24576 | tf_op jit(solution)/shard_map/jit(take_along_axis)/gather | solution.py:30
  390.2 2.7 fusion.16
  392.9 99.9 %all-to-all-done.1 = bf16[32,40,2048]{2,1,0:T(8,128)(2,1)} async-done(((bf16[32,40,2048]{2,1,0:T(8,128)(2,1)}), bf16[32,40,2048]{2,1,0:T(8,128)(2,1)}, u32[]{:S(2)}, u32[]{:S(2)}) %all-to-all-start.1) | async-done | bytes 5242912 | tf_op jit(solution)/shard_map/all_to_all | solution.py:90
  492.8 15.8 %gather_fusion.1 = bf16[1536,2048]{1,0:T(8,128)(2,1)} fusion(bf16[1280,2048]{1,0:T(8,128)(2,1)} %bitcast.11, s32[2048]{0:T(1024)S(1)} %pad_clamp_fusion.1), kind=kCustom, calls=%fused_computation.1 | custom fusion | bytes 12589056 | tf_op jit(solution)/shard_map/gather | solution.py:97
  508.7 10.9 %reshape.230 = bf16[256,6,2048]{2,1,0:T(8,128)(2,1)} reshape(bf16[1536,2048]{1,0:T(8,128)(2,1)} %gather_fusion.1) | data formatting | bytes 12582912 | tf_op jit(solution)/shard_map/gather | solution.py:97
  519.6 7.1 %fusion.78 = f32[256,1,2048]{2,1,0:T(1,128)} fusion(bf16[256,6,2048]{2,1,0:T(8,128)(2,1)} %reshape.230, bf16[256,6,1]{1,2,0:T(2,128)(2,1)S(1)} %copy.50), kind=kOutput, calls=%fused_computation.124 | convolution fusion | flops 6291456 | bytes 8391680 | tf_op jit(solution)/shard_map/tkd,tk->td/dot_general | solution.py:98
  526.7 5.9 fusion.6
  532.6 0.8 dynamic_slice.12
  533.4 51.3 %reduce-scatter.2.cloned.1.call-done = bf16[256,256]{1,0:T(8,128)(2,1)} async-done(((bf16[256,2048]{1,0:T(8,128)(2,1)}), bf16[256,256]{1,0:T(8,128)(2,1)}) %reduce-scatter.2.cloned.1.call-update) | async-done | bytes 131088 | tf_op jit(solution)/shard_map/reduce_scatter | solution.py:107
  584.7 1.0 fusion.47
  585.7 14.9 %psum.15 = f32[256]{0:T(256)S(1)} all-reduce(f32[256]{0:T(256)S(1)} %get-tuple-element.2), channel_id=1, replica_groups=mesh['ep'=32,'tp'=8] {'tp'}, use_global_device_ids=true, to_apply=%region_9.10 | all-reduce | flops 256 | bytes 2048 | tf_op jit(solution)/shard_map/psum | solution.py:113
  600.6 0.8 fusion.49
  (51 shorter events, 3.0 us)
Async XLA Ops:
  7.2 348.5 %copy-start = (bf16[1,352,2048]{2,1,0:T(8,128)(2,1)S(1)}, bf16[1,352,2048]{2,1,0:T(8,128)(2,1)}, u32[]{:S(2)}) copy-start(bf16[1,352,2048]{2,1,0:T(8,128)(2,1)} %param.18) | copy-start | bytes 4325380
  7.2 3.2 copy-start.4
  7.2 76.2 %all-reduce.2.cloned.1.call-start = ((), (), s32[]{:S(2)}) async-start(), calls=%async_computation.3 | async-start | bytes 4194304 | tf_op jit(solution)/shard_map/psum | solution.py:50
  83.4 2.3 copy-start.5
  106.9 241.7 %all-to-all-start = ((bf16[32,2,40,2048]{3,2,1,0:T(8,128)(2,1)}), bf16[32,2,40,2048]{3,2,1,0:T(8,128)(2,1)}, u32[]{:S(2)}, u32[]{:S(2)}) async-start(bf16[32,2,40,2048]{3,2,1,0:T(8,128)(2,1)} %broadcast_select_fusion), calls=%async_computation | async-start | bytes 20971520 | tf_op jit(solution)/shard_map/all_to_all | solution.py:75
  365.5 11.1 %copy-start.3 = (bf16[2048,64]{0,1:T(8,128)(2,1)S(1)}, bf16[2048,64]{0,1:T(8,128)(2,1)}, u32[]{:S(2)}) copy-start(bf16[2048,64]{0,1:T(8,128)(2,1)} %param.16) | copy-start | bytes 786436
  365.5 127.3 %all-to-all-start.1 = ((bf16[32,40,2048]{2,1,0:T(8,128)(2,1)}), bf16[32,40,2048]{2,1,0:T(8,128)(2,1)}, u32[]{:S(2)}, u32[]{:S(2)}) async-start(bf16[32,40,2048]{2,1,0:T(8,128)(2,1)} %convolution_convert_fusion), calls=%async_computation.1 | async-start | bytes 10485760 | tf_op jit(solution)/shard_map/all_to_all | solution.py:90
  375.7 209.0 %reduce-scatter.2.cloned.1.call-start = ((), (), s32[]{:S(2)}) async-start(), calls=%async_computation.4 | async-start | bytes 1179648 | tf_op jit(solution)/shard_map/reduce_scatter | solution.py:107
  526.7 74.7 %copy-start.1 = (bf16[1,352,2048]{2,1,0:T(8,128)(2,1)S(1)}, bf16[1,352,2048]{2,1,0:T(8,128)(2,1)}, u32[]{:S(2)}) copy-start(bf16[1,352,2048]{2,1,0:T(8,128)(2,1)} %param.18) | copy-start | bytes 4325380
  585.7 15.7 %copy-start.2 = (bf16[256,256]{1,0:T(8,128)(2,1)}, bf16[256,256]{1,0:T(8,128)(2,1)S(1)}, u32[]{:S(2)}) copy-start(bf16[256,256]{1,0:T(8,128)(2,1)S(1)} %get-tuple-element.3) | copy-start | bytes 393220
Sparse Core Ops, SparseCore 0:
  10.5 72.8 all-reduce.1
  532.7 51.9 reduce-scatter.1
where the time goes:
time: 609 us; the launch traced here: 608 us
  waiting for transfers between devices  427 us (70%)
  local copies, waits for them, and re-layouts  60.9 us (10%)
  matrix products  36.1 us (6%)
  other arithmetic  33.8 us (6%)
  starting transfers between devices  20.1 us (3%)
  between operations  15 us (2%)
  blocking collectives  14.9 us (2%)
    all_to_all x1, waiting for transfers between devices, on_device(): lax.all_to_all(dispatched, 'ep', split_axis=0, concat_axis=0, tiled=True)  232 us
    all_to_all x1, waiting for transfers between devices, on_device(): lax.all_to_all(produced, 'ep', split_axis=0, concat_axis=0, tiled=True)  99.9 us
    reduce_scatter x1, waiting for transfers between devices, on_device(): lax.psum_scatter((routed_part + shared_part).astype(jnp.bfloat16), 'tp',...  51.3 us
    psum x1, waiting for transfers between devices, on_device(): summed = lax.psum(partial_out, 'tp')  44.1 us
    gather x2, local copies, waits for them, and re-layouts, on_device(): picked = flat_terms[term_row]  26.8 us
    another operation x3, other arithmetic  18.4 us
    psum x1, blocking collectives, on_device(): squares = lax.psum(jnp.sum(next_wide * next_wide, axis=1), 'tp')  14.9 us
    gather x5, local copies, waits for them, and re-layouts, gate_weights(): chosen = jnp.take_along_axis(logits, route_block, axis=1)  13.2 us
  transfers between devices with their start and end apart: 4, of which 4 were waited for; matrix products, arithmetic and copies ran while one was open for 8% of the time, Pallas kernels for 0%

commit v1 on v0

--- a/solution.py
+++ b/solution.py
@@ -2,6 +2,7 @@
 import jax.numpy as jnp
 from jax import lax
 from jax.sharding import PartitionSpec as P
+from jax.lax import axis_size, ppermute
 
 EXP_DEV = 2
 norm_epsilon = 1e-06
@@ -47,7 +48,17 @@
     next_gain,
 ):
     partial_out = jnp.dot(attn_out, out_proj, preferred_element_type=jnp.float32)
-    summed = lax.psum(partial_out, "tp")
+
+    def connect_signs_over_axis(panel, named_axis):
+        sides = axis_size(named_axis)
+        even = panel
+        for dev in [no for no in (1, 2, 4, 8, 16) if no < sides]:
+            even = even + ppermute(
+                even, axis_name=named_axis, perm=[(dev_j, dev_j ^ dev) for dev_j in range(sides)]
+            )
+        return even
+
+    summed = connect_signs_over_axis(partial_out, "tp")
     stream = (summed + residual.astype(jnp.float32)).astype(jnp.bfloat16)
     stream_wide = stream.astype(jnp.float32)
     normed = (

time: 609 us -> 659 us (1.082)
  other arithmetic: 33.8 us -> 60.8 us
  local copies, waits for them, and re-layouts: 60.9 us -> 78.6 us
  starting transfers between devices: 20.1 us -> 33.4 us
  waiting for transfers between devices: 427 us -> 419 us
    ppermute x0 -> x3, waiting for transfers between devices: none -> 50.6 us  [connect_signs_over_axis(): ppermute(even, axis_name=named_axis, perm=[(dev_j, dev_j ^ dev) for dev_j...]
    psum x1 -> x0, waiting for transfers between devices: 44.1 us -> none  [on_device(): summed = lax.psum(partial_out, 'tp')]
    reduce_scatter x1, waiting for transfers between devices: 51.3 us -> 31.3 us  [on_device(): lax.psum_scatter((routed_part + shared_part).astype(jnp.bfloat16), 'tp',...]
    another operation x3, other arithmetic: 18.4 us -> 36.4 us
    all_to_all x1, starting transfers between devices: 10.2 us -> 17.1 us  [on_device(): lax.all_to_all(produced, 'ep', split_axis=0, concat_axis=0, tiled=True)]
  transfers between devices with their start and end apart: 4 -> 6, of which waited for: 4 -> 5; matrix products, arithmetic and copies ran while one was open for 8% -> 13% of each run, Pallas kernels for 0% -> 0%
where the time goes in v1:
time: 659 us; the launch traced here: 655 us
  waiting for transfers between devices  419 us (64%)
  local copies, waits for them, and re-layouts  78.6 us (12%)
  other arithmetic  60.8 us (9%)
  matrix products  34 us (5%)
  starting transfers between devices  33.4 us (5%)
  between operations  15 us (2%)
  blocking collectives  14.9 us (2%)
    all_to_all x1, waiting for transfers between devices, on_device(): lax.all_to_all(dispatched, 'ep', split_axis=0, concat_axis=0, tiled=True)  238 us
    all_to_all x1, waiting for transfers between devices, on_device(): lax.all_to_all(produced, 'ep', split_axis=0, concat_axis=0, tiled=True)  99 us
    ppermute x3, waiting for transfers between devices, connect_signs_over_axis(): ppermute(even, axis_name=named_axis, perm=[(dev_j, dev_j ^ dev) for dev_j...  50.6 us
    another operation x3, other arithmetic  36.4 us
    reduce_scatter x1, waiting for transfers between devices, on_device(): lax.psum_scatter((routed_part + shared_part).astype(jnp.bfloat16), 'tp',...  31.3 us
    gather x2, local copies, waits for them, and re-layouts, on_device(): picked = flat_terms[term_row]  26.8 us
    all_to_all x1, starting transfers between devices, on_device(): lax.all_to_all(produced, 'ep', split_axis=0, concat_axis=0, tiled=True)  17.1 us
    psum x1, blocking collectives, on_device(): squares = lax.psum(jnp.sum(next_wide * next_wide, axis=1), 'tp')  14.9 us
  transfers between devices with their start and end apart: 6, of which 5 were waited for; matrix products, arithmetic and copies ran while one was open for 13% of the time, Pallas kernels for 0%

profile of v1, /device:TPU:1, one launch (start us, length us, event | category | flops | bytes accessed | tf_op | source)
XLA Modules:
  0.0 655.4 jit_solution(11748817112359304546)
XLA Ops:
  7.2 1.8 fusion.67
  9.0 3.3 collective-permute-start
  12.3 3.8 collective-permute-done
  16.6 46.8 %collective-permute-done.1 = f32[256,2048]{1,0:T(8,128)S(1)} collective-permute-done((f32[256,2048]{1,0:T(8,128)S(1)}, f32[256,2048]{1,0:T(8,128)S(1)}, u32[]{:S(2)}, u32[]{:S(2)}) %collective-permute-start.1) | collective-permute-done | bytes 2097184 | tf_op jit(solution)/shard_map/ppermute | solution.py:56
  66.8 1.6 eq.33
  70.0 34.5 %reduce-window.6 = s32[64,12,128]{2,1,0:T(8,128)} reduce-window(s32[64,12,128]{2,1,0:T(8,128)} %fusion.29, s32[]{:T(128)} %constant.103.clone.1), window={size=1x1x128 pad=0_0x0_0x127_0}, to_apply=%region_0.0 | reduce-window | flops 12484608 | bytes 786436 | tf_op jit(solution)/shard_map/reduce-window
  104.5 2.1 slice.30
  108.4 1.4 copy.45
  112.8 1.6 copy.46
  115.7 1.5 copy.41
  117.2 1.6 mul.91
  120.1 6.9 %scatter_custom_fusion = s32[2560]{0:T(1024)} fusion(s32[1536]{0:T(1024)} %fusion.58, s32[1536]{0:T(1024)S(1)} %iota.72, s32[]{:T(128)} %constant.107.clone.1), kind=kCustom, calls=%fused_computation.106 | custom fusion | bytes 10752 | tf_op jit(solution)/shard_map/scatter | solution.py:24
  130.5 1.4 div.89
  132.6 1.5 compare_select_fusion
  134.1 1.5 reshape.223
  136.8 2.4 fusion.7
  140.6 10.8 %gather_fusion = bf16[2560,2048]{1,0:T(8,128)(2,1)} fusion(bf16[256,2048]{1,0:T(8,128)(2,1)S(1)} %fusion.9, s32[3072]{0:T(1024)S(1)} %copy-done.6), kind=kCustom, calls=%fused_computation | custom fusion | bytes 20981760 | tf_op jit(solution)/shard_map/gather | solution.py:84
  151.4 10.0 %broadcast_select_fusion = bf16[32,2,40,2048]{3,2,1,0:T(8,128)(2,1)} fusion(bf16[32,2,40,2048]{3,2,1,0:T(8,128)(2,1)} %bitcast.81, pred[32,2,40]{2,1,0:T(4,128)(4,1)S(1)} %copy-done.7), kind=kLoop, calls=%fused_computation.4 | loop fusion | flops 5242880 | bytes 20974080 | tf_op jit(solution)/shard_map/jit(_where)/select_n | solution.py:84
  161.3 11.3 %all-to-all-start = ((bf16[32,2,40,2048]{3,2,1,0:T(8,128)(2,1)}), bf16[32,2,40,2048]{3,2,1,0:T(8,128)(2,1)}, u32[]{:S(2)}, u32[]{:S(2)}) async-start(bf16[32,2,40,2048]{3,2,1,0:T(8,128)(2,1)} %broadcast_select_fusion), calls=%async_computation | async-start | bytes 20971520 | tf_op jit(solution)/shard_map/all_to_all | solution.py:86
  172.7 237.8 %all-to-all-done = bf16[32,2,40,2048]{3,2,1,0:T(8,128)(2,1)} async-done(((bf16[32,2,40,2048]{3,2,1,0:T(8,128)(2,1)}), bf16[32,2,40,2048]{3,2,1,0:T(8,128)(2,1)}, u32[]{:S(2)}, u32[]{:S(2)}) %all-to-all-start) | async-done | bytes 10485792 | tf_op jit(solution)/shard_map/all_to_all | solution.py:86
  410.4 7.1 %fusion.2 = f32[32,40,352]{2,1,0:T(8,128)} fusion(bf16[32,2,40,2048]{3,2,1,0:T(8,128)(2,1)} %all-to-all-done, s32[]{:T(128)S(6)} %select_n.135, bf16[1,2,352,2048]{3,2,1,0:T(8,128)(2,1)} %param.17), kind=kOutput, calls=%fused_computation.7 | convolution fusion | flops 1845493760 | bytes 8486916 | tf_op jit(solution)/shard_map/scd,fd->scf/dot_general | solution.py:91
  417.6 9.8 %convolution_convert_fusion = bf16[32,40,2048]{2,1,0:T(8,128)(2,1)} fusion(bf16[1,352,2048]{2,1,0:T(8,128)(2,1)S(1)} %copy-done, f32[32,40,352]{2,1,0:T(8,128)} %fusion.2, bf16[32,2,40,2048]{3,2,1,0:T(8,128)(2,1)} %all-to-all-done, s32[]{:T(128)S(6)} %select_n.135, bf16[1,2,352,2048]{3,2,1,0:T(8,128)(2,1)} %param.17), kind=kOutput, calls=%fused_computation.11 | convolution fusion | flops 3696312320 | bytes 15335428 | tf_op jit(solution)/shard_map/scf,fd->scd/dot_general | solution.py:98
  427.3 17.1 %all-to-all-start.1 = ((bf16[32,40,2048]{2,1,0:T(8,128)(2,1)}), bf16[32,40,2048]{2,1,0:T(8,128)(2,1)}, u32[]{:S(2)}, u32[]{:S(2)}) async-start(bf16[32,40,2048]{2,1,0:T(8,128)(2,1)} %convolution_convert_fusion), calls=%async_computation.1 | async-start | bytes 10485760 | tf_op jit(solution)/shard_map/all_to_all | solution.py:101
  445.8 12.7 %gather_fusion.2 = f32[1536]{0:T(1024)S(1)} fusion(f32[256,64]{0,1:T(8,128)S(1)} %fusion.68, s32[1536]{0:T(1024)S(1)} %reshape.237), kind=kCustom, calls=%fused_computation.2 | custom fusion | bytes 24576 | tf_op jit(solution)/shard_map/jit(take_along_axis)/gather | solution.py:31
  459.0 1.9 fusion.14
  460.9 99.0 %all-to-all-done.1 = bf16[32,40,2048]{2,1,0:T(8,128)(2,1)} async-done(((bf16[32,40,2048]{2,1,0:T(8,128)(2,1)}), bf16[32,40,2048]{2,1,0:T(8,128)(2,1)}, u32[]{:S(2)}, u32[]{:S(2)}) %all-to-all-start.1) | async-done | bytes 5242912 | tf_op jit(solution)/shard_map/all_to_all | solution.py:101
  559.9 15.8 %gather_fusion.1 = bf16[1536,2048]{1,0:T(8,128)(2,1)} fusion(bf16[1280,2048]{1,0:T(8,128)(2,1)} %bitcast.11, s32[2048]{0:T(1024)S(1)} %pad_clamp_fusion.1), kind=kCustom, calls=%fused_computation.1 | custom fusion | bytes 12589056 | tf_op jit(solution)/shard_map/gather | solution.py:108
  575.8 10.9 %reshape.230 = bf16[256,6,2048]{2,1,0:T(8,128)(2,1)} reshape(bf16[1536,2048]{1,0:T(8,128)(2,1)} %gather_fusion.1) | data formatting | bytes 12582912 | tf_op jit(solution)/shard_map/gather | solution.py:108
  586.7 7.1 %fusion.69 = f32[256,1,2048]{2,1,0:T(1,128)} fusion(bf16[256,6,2048]{2,1,0:T(8,128)(2,1)} %reshape.230, bf16[256,6,1]{1,2,0:T(2,128)(2,1)S(1)} %copy.50), kind=kOutput, calls=%fused_computation.118 | convolution fusion | flops 6291456 | bytes 8391680 | tf_op jit(solution)/shard_map/tkd,tk->td/dot_general | solution.py:109
  593.8 5.8 fusion.6
  600.4 31.3 %reduce-scatter.2.cloned.1.call-done = bf16[256,256]{1,0:T(8,128)(2,1)} async-done(((bf16[256,2048]{1,0:T(8,128)(2,1)}), bf16[256,256]{1,0:T(8,128)(2,1)}) %reduce-scatter.2.cloned.1.call-update) | async-done | bytes 131088 | tf_op jit(solution)/shard_map/reduce_scatter | solution.py:118
  632.8 14.9 %psum.7 = f32[256]{0:T(256)S(1)} all-reduce(f32[256]{0:T(256)S(1)} %get-tuple-element.2), channel_id=1, replica_groups=mesh['ep'=32,'tp'=8] {'tp'}, use_global_device_ids=true, to_apply=%region_8.9 | all-reduce | flops 256 | bytes 2048 | tf_op jit(solution)/shard_map/psum | solution.py:124
  (64 shorter events, 23.3 us)
Async XLA Ops:
  7.2 410.4 %copy-start = (bf16[1,352,2048]{2,1,0:T(8,128)(2,1)S(1)}, bf16[1,352,2048]{2,1,0:T(8,128)(2,1)}, u32[]{:S(2)}) copy-start(bf16[1,352,2048]{2,1,0:T(8,128)(2,1)} %param.18) | copy-start | bytes 4325380
  9.0 7.1 %collective-permute-start = (f32[256,2048]{1,0:T(8,128)S(1)}, f32[256,2048]{1,0:T(8,128)S(1)}, u32[]{:S(2)}, u32[]{:S(2)}) collective-permute-start(f32[256,2048]{1,0:T(8,128)S(1)} %fusion.67), channel_id=1, source_target_pairs={{0,1},{1,0},{2,3},{3,2},{4,5},{5,4},{6,7},{7,6},{8,9},{9,8},{10,11... | collective-permute-start | bytes 6291464 | tf_op jit(solution)/shard_map/ppermute | solution.py:56
  16.5 48.5 %copy-start.5 = (s32[256,6]{0,1:T(8,128)S(1)}, s32[256,6]{0,1:T(8,128)}, u32[]{:S(2)}) copy-start(s32[256,6]{0,1:T(8,128)} %param.21) | copy-start | bytes 18436
  16.5 46.9 %collective-permute-start.1 = (f32[256,2048]{1,0:T(8,128)S(1)}, f32[256,2048]{1,0:T(8,128)S(1)}, u32[]{:S(2)}, u32[]{:S(2)}) collective-permute-start(f32[256,2048]{1,0:T(8,128)S(1)} %add.146), channel_id=1, source_target_pairs={{0,2},{1,3},{2,0},{3,1},{4,6},{5,7},{6,4},{7,5},{8,10},{9,11},{10,... | collective-permute-start | bytes 6291464 | tf_op jit(solution)/shard_map/ppermute | solution.py:56
  63.7 73.1 %collective-permute-start.2 = (f32[256,2048]{1,0:T(8,128)S(1)}, f32[256,2048]{1,0:T(8,128)}, u32[]{:S(2)}, u32[]{:S(2)}) collective-permute-start(f32[256,2048]{1,0:T(8,128)S(1)} %add.147), channel_id=1, source_target_pairs={{0,4},{1,5},{2,6},{3,7},{4,0},{5,1},{6,2},{7,3},{8,12},{9,13},{10,... | collective-permute-start | bytes 6291464 | tf_op jit(solution)/shard_map/ppermute | solution.py:56
  136.8 3.4 copy-start.9
  139.3 1.0 copy-start.2
  139.3 1.3 copy-start.6
  140.6 10.8 %copy-start.7 = (pred[32,2,40]{2,1,0:T(4,128)(4,1)S(1)}, pred[32,2,40]{2,1,0:T(4,128)(4,1)}, u32[]{:S(2)}) copy-start(pred[32,2,40]{2,1,0:T(4,128)(4,1)} %ge.27) | copy-start | bytes 7684
  161.3 249.1 %all-to-all-start = ((bf16[32,2,40,2048]{3,2,1,0:T(8,128)(2,1)}), bf16[32,2,40,2048]{3,2,1,0:T(8,128)(2,1)}, u32[]{:S(2)}, u32[]{:S(2)}) async-start(bf16[32,2,40,2048]{3,2,1,0:T(8,128)(2,1)} %broadcast_select_fusion), calls=%async_computation | async-start | bytes 20971520 | tf_op jit(solution)/shard_map/all_to_all | solution.py:86
  427.3 17.4 %copy-start.8 = (s32[256,6]{0,1:T(8,128)S(1)}, s32[256,6]{0,1:T(8,128)}, u32[]{:S(2)}) copy-start(s32[256,6]{0,1:T(8,128)} %get-tuple-element.8) | copy-start | bytes 18436
  427.3 18.0 %copy-start.4 = (bf16[2048,64]{0,1:T(8,128)(2,1)S(1)}, bf16[2048,64]{0,1:T(8,128)(2,1)}, u32[]{:S(2)}) copy-start(bf16[2048,64]{0,1:T(8,128)(2,1)} %param.16) | copy-start | bytes 786436
  427.3 132.6 %all-to-all-start.1 = ((bf16[32,40,2048]{2,1,0:T(8,128)(2,1)}), bf16[32,40,2048]{2,1,0:T(8,128)(2,1)}, u32[]{:S(2)}, u32[]{:S(2)}) async-start(bf16[32,40,2048]{2,1,0:T(8,128)(2,1)} %convolution_convert_fusion), calls=%async_computation.1 | async-start | bytes 10485760 | tf_op jit(solution)/shard_map/all_to_all | solution.py:101
  444.4 187.3 %reduce-scatter.2.cloned.1.call-start = ((), (), s32[]{:S(2)}) async-start(), calls=%async_computation.3 | async-start | bytes 1179648 | tf_op jit(solution)/shard_map/reduce_scatter | solution.py:118
  593.8 54.7 %copy-start.1 = (bf16[1,352,2048]{2,1,0:T(8,128)(2,1)S(1)}, bf16[1,352,2048]{2,1,0:T(8,128)(2,1)}, u32[]{:S(2)}) copy-start(bf16[1,352,2048]{2,1,0:T(8,128)(2,1)} %param.18) | copy-start | bytes 4325380
  632.8 15.7 %copy-start.3 = (bf16[256,256]{1,0:T(8,128)(2,1)}, bf16[256,256]{1,0:T(8,128)(2,1)S(1)}, u32[]{:S(2)}) copy-start(bf16[256,256]{1,0:T(8,128)(2,1)S(1)} %get-tuple-element.3) | copy-start | bytes 393220
Sparse Core Ops, SparseCore 0:
  599.8 31.9 reduce-scatter.1
